TPU v7x, 512 devices: a whole 4x4x16 slice. The times are simulated.
512 devices in a mesh: dp: 512 (over z, x, y, core).
Axes of the slice: x: 4, y: 4, z: 16, core: 2. Of those that a mesh axis runs over, the one named last changes fastest.
Arguments:
- inputs: bfloat16 [2048, 199, 512], P('dp'), may hold values from -6 to 6
- weights: bfloat16 [2, 262144], replicated, may hold values from -0.1875 to 0.1875
- ln_gain: float32 [512], replicated, may hold values from 0.45 to 2.16
- ln_bias: float32 [512], replicated, may hold values from -3 to 3
- projection: bfloat16 [512, 1024], replicated, may hold values from -0.25 to 0.25
- targets: float32 [2048, 1024], P('dp'), may hold values from -6 to 6
- master: float32 [2, 262144], P(None, 'dp'), may hold values from -0.006 to 0.006
- first_moment: float32 [2, 262144], P(None, 'dp'), may hold values from -0.0006 to 0.0006
- second_moment: float32 [2, 262144], P(None, 'dp'), may hold values from 1e-11 to 1e-08
Outputs:
- input_grad: bfloat16 [2048, 199, 512], P('dp')
- update: float32 [2, 262144], P(None, 'dp')
- new_master: float32 [2, 262144], P(None, 'dp')
- new_first: float32 [2, 262144], P(None, 'dp')
- new_second: float32 [2, 262144], P(None, 'dp')
- new_weights: bfloat16 [2, 262144], replicated
All inputs are finite; a program needn't handle non-finite values.
Results may differ from a plain program's by a relative error of at most 0.006.
Values may be sent and summed in bfloat16 or wider, within the bound.
No kernel may reach another device: no remote copies, remote signals or barrier semaphores. Data moves between devices by JAX's collectives and lax.ppermute only.
A program may use at most 64 MiB of HBM per device.

v0:
```python
import jax
import jax.numpy as jnp
from jax import lax
from jax.sharding import PartitionSpec as P


def norm_act(pre, gain, bias):
    center = pre - jnp.mean(pre, axis=-1, keepdims=True)
    spread = jnp.mean(center * center, axis=-1, keepdims=True)
    normed = center * lax.rsqrt(spread + 1e-05)
    return jax.nn.gelu(normed * gain + bias, approximate=False)


def local_pass(inputs, weights, ln_gain, ln_bias, projection, targets):
    clips, frames_in, chans = inputs.shape
    taps = weights.shape[0]
    frames_out = (frames_in - taps) // taps + 1
    windows = inputs[:, : frames_out * taps].reshape(clips, frames_out, taps, chans)
    kernel = weights.reshape(taps, chans, chans)
    pre = jnp.einsum("bfki,koi->bfo", windows, kernel, preferred_element_type=jnp.float32)
    act, pull = jax.vjp(lambda value: norm_act(value, ln_gain, ln_bias), pre)
    pooled = jnp.mean(act, axis=1).astype(jnp.bfloat16)
    predicted = jnp.dot(pooled, projection, preferred_element_type=jnp.float32)
    miss = (predicted - targets).astype(jnp.bfloat16)
    back = lax.dot_general(
        miss, projection, (((1,), (1,)), ((), ())), preferred_element_type=jnp.float32
    )
    upstream = jnp.broadcast_to(back[:, None, :] / frames_out, act.shape)
    dpre = pull(upstream)[0].astype(jnp.bfloat16)
    dwin = jnp.einsum("bfo,koi->bfki", dpre, kernel, preferred_element_type=jnp.float32).astype(
        jnp.bfloat16
    )
    dinput = dwin.reshape(clips, frames_out * taps, chans)
    tail = jnp.zeros((clips, frames_in - frames_out * taps, chans), jnp.bfloat16)
    return (windows, dpre, jnp.concatenate([dinput, tail], axis=1))


def body(
    inputs, weights, ln_gain, ln_bias, projection, targets, master, first_moment, second_moment
):
    windows, dpre, input_grad = local_pass(inputs, weights, ln_gain, ln_bias, projection, targets)
    taps = weights.shape[0]
    term = jnp.einsum("bfo,bfki->koi", dpre, windows, preferred_element_type=jnp.float32)
    grad = lax.psum_scatter(term.reshape(taps, -1), "dp", scatter_dimension=1, tiled=True)
    squares = lax.psum(jnp.sum(grad * grad), "dp")
    scale = jnp.minimum(1.0, 1.0 / (jnp.sqrt(squares) + 1e-06))
    clipped = scale * grad
    new_first = 0.9 * first_moment + 0.1 * clipped
    new_second = 0.999 * second_moment + 0.001 * clipped * clipped
    update = new_first / (1.0 - 0.9**20) / (jnp.sqrt(new_second / (1.0 - 0.999**20)) + 1e-08)
    new_master = master - 0.0001 * (update + 0.01 * master)
    new_weights = lax.all_gather(new_master.astype(jnp.bfloat16), "dp", axis=1, tiled=True)
    return (input_grad, update, new_master, new_first, new_second, new_weights)


def solution(mesh):
    return jax.shard_map(
        body,
        mesh=mesh,
        in_specs=(
            P("dp", None, None),
            P(),
            P(),
            P(),
            P(),
            P("dp", None),
            P(None, "dp"),
            P(None, "dp"),
            P(None, "dp"),
        ),
        out_specs=(
            P("dp", None, None),
            P(None, "dp"),
            P(None, "dp"),
            P(None, "dp"),
            P(None, "dp"),
            P(),
        ),
        check_vma=False,
    )
```

profile of v0, /device:TPU:1, one launch (start us, length us, event | category | flops | bytes accessed | tf_op | source)
XLA Modules:
  0.0 786.2 jit_solution(7399412350724682430)
XLA Ops:
  7.2 0.0 copy-start
  7.2 0.0 all-reduce.4.cloned.1.call-start
  7.2 1.5 slice.3
  8.7 0.0 copy-start.1
  8.7 0.0 copy-start.5
  8.8 0.0 copy-start.6
  8.8 2.3 fusion.26
  11.1 0.0 copy-start.7
  11.1 0.3 multiply_reduce_fusion.2
  11.3 0.0 copy-done.1
  11.4 0.0 copy-done.5
  11.4 0.0 copy-done.6
  11.4 2.2 multiply_reduce_fusion.1
  13.6 0.0 copy-done
  13.6 0.0 copy-done.7
  13.6 0.5 broadcast_multiply_fusion
  14.1 0.0 copy-start.2
  14.1 0.7 multiply_reduce_fusion
  14.9 0.8 fusion.24
  15.7 0.0 copy-start.3
  15.8 0.9 copy-done.3
  16.6 0.0 copy-done.2
  16.6 0.9 convolution_bitcast_fusion
  17.5 2.9 copy.28
  20.5 0.0 copy-start.8
  20.5 0.0 copy-start.9
  20.5 0.0 copy-start.10
  20.5 0.0 copy-start.4
  20.5 0.0 copy-start.11
  20.5 0.0 all-reduce.4.cloned.1.call-update
  20.5 0.0 all-gather.2.cloned.1.call-start
  20.6 487.3 %all-reduce.4.cloned.1.call-done = f32[2,262144]{1,0:T(2,128)} async-done(((f32[2,262144]{1,0:T(2,128)}), f32[2,262144]{1,0:T(2,128)}) %all-reduce.4.cloned.1.call-update) | async-done | bytes 2097168
  507.8 1.3 multiply_reduce_fusion.3
  509.1 103.3 %psum.7 = f32[]{:T(128)} all-reduce(f32[]{:T(128)} %multiply_reduce_fusion.3), channel_id=1, replica_groups=mesh['dp'=512] {'dp'}, use_global_device_ids=true, to_apply=%region_7.0 | all-reduce | flops 1 | bytes 8 | tf_op jit(solution)/shard_map/psum | solution.py:45
  613.2 0.0 copy-done.8
  613.2 0.0 copy-done.9
  613.2 0.0 copy-done.10
  613.2 1.3 fusion.22
  614.5 0.0 all-gather.2.cloned.1.call-update
  614.5 0.0 copy-done.4
  614.5 0.0 copy-done.11
  614.6 0.7 convolution_convert_fusion
  615.2 0.6 copy.20
  615.9 1.2 concatenate.3
  617.1 159.7 %all-gather.2.cloned.1.call-done = bf16[2,262144]{1,0:T(2,128)(2,1)} async-done(((bf16[2,512]{1,0:T(2,128)(2,1)}), bf16[2,262144]{1,0:T(2,128)(2,1)}) %all-gather.2.cloned.1.call-update) | async-done | bytes 1048592 | tf_op jit(solution)/shard_map/all_gather | solution.py:52
  776.8 2.6 copy.47
  (4 shorter events, 0.0 us)
Async XLA Ops:
  7.2 6.5 copy-start
  7.2 500.6 %all-reduce.4.cloned.1.call-start = ((), (), s32[]{:S(2)}) async-start(), calls=%async_computation.1 | async-start | bytes 4194304
  8.7 2.6 copy-start.1
  8.7 2.6 copy-start.5
  8.8 2.6 copy-start.6
  11.1 2.6 copy-start.7
  14.1 2.5 copy-start.2
  15.7 0.9 copy-start.3
  20.5 592.7 %copy-start.8 = (f32[2,512]{1,0:T(2,128)S(1)}, f32[2,512]{1,0:T(2,128)}, u32[]{:S(2)}) copy-start(f32[2,512]{1,0:T(2,128)} %param.15) | copy-start | bytes 12292
  20.5 592.7 %copy-start.9 = (f32[2,512]{1,0:T(2,128)S(1)}, f32[2,512]{1,0:T(2,128)}, u32[]{:S(2)}) copy-start(f32[2,512]{1,0:T(2,128)} %param.16) | copy-start | bytes 12292
  20.5 592.7 %copy-start.10 = (f32[2,512]{1,0:T(2,128)S(1)}, f32[2,512]{1,0:T(2,128)}, u32[]{:S(2)}) copy-start(f32[2,512]{1,0:T(2,128)} %param.17) | copy-start | bytes 12292
  20.5 594.1 %copy-start.4 = (f32[4,99,512]{2,1,0:T(8,128)S(1)}, f32[4,99,512]{2,1,0:T(8,128)}, u32[]{:S(2)}) copy-start(f32[4,99,512]{2,1,0:T(8,128)} %copy-done.3) | copy-start | bytes 2433028
  20.5 594.1 %copy-start.11 = (bf16[2,262144]{1,0:T(2,128)(2,1)S(1)}, bf16[2,262144]{1,0:T(2,128)(2,1)}, u32[]{:S(2)}) copy-start(bf16[2,262144]{1,0:T(2,128)(2,1)} %param.10) | copy-start | bytes 3145732
  20.5 756.3 %all-gather.2.cloned.1.call-start = ((), (), s32[]{:S(2)}) async-start(), calls=%async_computation | async-start | bytes 1050624 | tf_op jit(solution)/shard_map/all_gather | solution.py:52
Sparse Core Ops, SparseCore 0:
  20.6 487.1 all-reduce.3
  614.7 162.0 all-gather.1
where the time goes:
time: 787 us; the launch traced here: 786 us
  waiting for transfers between devices  647 us (82%)
  blocking collectives  103 us (13%)
  between operations  15 us (2%)
  local copies, waits for them, and re-layouts  9.76 us (1%)
    unnamed x3, waiting for transfers between devices  487 us
    all_gather x1, waiting for transfers between devices, body(): lax.all_gather(new_master.astype(jnp.bfloat16), 'dp', axis=1, tiled=True)  160 us
    psum x1, blocking collectives, body(): squares = lax.psum(jnp.sum(grad * grad), 'dp')  103 us
  transfers between devices with their start and end apart: 2, of which 2 were waited for; matrix products, arithmetic and copies ran while one was open for 0% of the time, Pallas kernels for 0%

commit v1 on v0

--- a/solution.py
+++ b/solution.py
@@ -49,7 +49,12 @@
     new_second = 0.999 * second_moment + 0.001 * clipped * clipped
     update = new_first / (1.0 - 0.9**20) / (jnp.sqrt(new_second / (1.0 - 0.999**20)) + 1e-08)
     new_master = master - 0.0001 * (update + 0.01 * master)
-    new_weights = lax.all_gather(new_master.astype(jnp.bfloat16), "dp", axis=1, tiled=True)
+    new_weights = jnp.concatenate(
+        lax.all_to_all(
+            jnp.stack([new_master.astype(jnp.bfloat16)] * lax.axis_size("dp")), "dp", 0, 0
+        ),
+        axis=1,
+    )
     return (input_grad, update, new_master, new_first, new_second, new_weights)
 
 

time: 787 us -> 695 us (0.88)
  waiting for transfers between devices: 647 us -> 542 us
  starting transfers between devices: 0.08 us -> 12.5 us
    all_gather x1 -> x0, waiting for transfers between devices: 160 us -> none  [body(): lax.all_gather(new_master.astype(jnp.bfloat16), 'dp', axis=1, tiled=True)]
    all_to_all x0 -> x1, waiting for transfers between devices: none -> 54.4 us  [body(): lax.all_to_all(jnp.stack([new_master.astype(jnp.bfloat16)] * lax.axis_siz...]
    all_to_all x0 -> x1, starting transfers between devices: none -> 12.5 us  [body(): lax.all_to_all(jnp.stack([new_master.astype(jnp.bfloat16)] * lax.axis_siz...]
    unnamed x3 -> x2, waiting for transfers between devices: 487 us -> 487 us
  transfers between devices with their start and end apart: 2 -> 2, of which waited for: 2 -> 2; matrix products, arithmetic and copies ran while one was open for 0% -> 1% of each run, Pallas kernels for 0% -> 0%
where the time goes in v1:
time: 695 us; the launch traced here: 694 us
  waiting for transfers between devices  542 us (78%)
  blocking collectives  103 us (15%)
  between operations  15 us (2%)
  starting transfers between devices  12.5 us (2%)
  local copies, waits for them, and re-layouts  9.67 us (1%)
    unnamed x2, waiting for transfers between devices  487 us
    psum x1, blocking collectives, body(): squares = lax.psum(jnp.sum(grad * grad), 'dp')  103 us
    all_to_all x1, waiting for transfers between devices, body(): lax.all_to_all(jnp.stack([new_master.astype(jnp.bfloat16)] * lax.axis_siz...  54.4 us
  transfers between devices with their start and end apart: 2, of which 2 were waited for; matrix products, arithmetic and copies ran while one was open for 1% of the time, Pallas kernels for 0%

profile of v1, /device:TPU:1, one launch (start us, length us, event | category | flops | bytes accessed | tf_op | source)
XLA Modules:
  0.0 694.4 jit_solution(4244503967939782309)
XLA Ops:
  7.2 0.0 copy-start
  7.2 0.0 all-reduce.4.cloned.1.call-start
  7.2 1.5 slice.3
  8.7 0.0 copy-start.1
  8.7 0.0 copy-start.5
  8.8 0.0 copy-start.6
  8.8 2.3 fusion.26
  11.1 0.0 copy-start.7
  11.1 0.3 multiply_reduce_fusion.2
  11.3 0.0 copy-done.1
  11.4 0.0 copy-done.5
  11.4 0.0 copy-done.6
  11.4 2.2 multiply_reduce_fusion.1
  13.6 0.0 copy-done
  13.6 0.0 copy-done.7
  13.6 0.5 broadcast_multiply_fusion
  14.1 0.0 copy-start.2
  14.1 0.7 multiply_reduce_fusion
  14.9 0.8 fusion.24
  15.7 0.0 copy-start.3
  15.8 0.9 copy-done.3
  16.6 0.0 copy-done.2
  16.6 0.9 convolution_bitcast_fusion
  17.5 2.9 copy.28
  20.4 0.0 copy-start.8
  20.5 0.0 copy-start.9
  20.5 0.0 copy-start.10
  20.5 0.0 all-reduce.4.cloned.1.call-update
  20.5 0.0 copy-start.4
  20.5 487.3 %all-reduce.4.cloned.1.call-done = f32[2,262144]{1,0:T(2,128)} async-done(((f32[2,262144]{1,0:T(2,128)}), f32[2,262144]{1,0:T(2,128)}) %all-reduce.4.cloned.1.call-update) | async-done | bytes 2097168
  507.8 1.3 multiply_reduce_fusion.3
  509.1 103.3 %psum.7 = f32[]{:T(128)} all-reduce(f32[]{:T(128)} %multiply_reduce_fusion.3), channel_id=1, replica_groups=mesh['dp'=512] {'dp'}, use_global_device_ids=true, to_apply=%region_7.0 | all-reduce | flops 1 | bytes 8 | tf_op jit(solution)/shard_map/psum | solution.py:45
  613.1 0.0 copy-done.8
  613.2 0.0 copy-done.9
  613.2 0.0 copy-done.10
  613.2 1.3 fusion.22
  614.5 1.5 stack.2
  616.0 12.5 %all-to-all-start = ((bf16[512,2,512]{2,1,0:T(2,128)(2,1)}), bf16[512,2,512]{2,1,0:T(2,128)(2,1)S(1)}, u32[]{:S(2)}, u32[]{:S(2)}) async-start(bf16[512,2,512]{2,1,0:T(2,128)(2,1)} %stack.2), calls=%async_computation | async-start | bytes 2097152 | tf_op jit(solution)/shard_map/all_to_all | solution.py:53
  628.5 0.0 copy-done.4
  628.5 1.9 convolution_convert_fusion
  630.4 0.6 copy.20
  631.0 1.2 concatenate.3
  632.2 54.4 %all-to-all-done = bf16[512,2,512]{2,1,0:T(2,128)(2,1)S(1)} async-done(((bf16[512,2,512]{2,1,0:T(2,128)(2,1)}), bf16[512,2,512]{2,1,0:T(2,128)(2,1)S(1)}, u32[]{:S(2)}, u32[]{:S(2)}) %all-to-all-start) | async-done | bytes 1048608 | tf_op jit(solution)/shard_map/all_to_all | solution.py:53
  686.6 1.0 copy.47
  (4 shorter events, 0.0 us)
Async XLA Ops:
  7.2 6.5 copy-start
  7.2 500.6 %all-reduce.4.cloned.1.call-start = ((), (), s32[]{:S(2)}) async-start(), calls=%async_computation.1 | async-start | bytes 4194304
  8.7 2.6 copy-start.1
  8.7 2.6 copy-start.5
  8.8 2.6 copy-start.6
  11.1 2.6 copy-start.7
  14.1 2.5 copy-start.2
  15.7 0.9 copy-start.3
  20.4 592.7 %copy-start.8 = (f32[2,512]{1,0:T(2,128)S(1)}, f32[2,512]{1,0:T(2,128)}, u32[]{:S(2)}) copy-start(f32[2,512]{1,0:T(2,128)} %param.15) | copy-start | bytes 12292
  20.5 592.7 %copy-start.9 = (f32[2,512]{1,0:T(2,128)S(1)}, f32[2,512]{1,0:T(2,128)}, u32[]{:S(2)}) copy-start(f32[2,512]{1,0:T(2,128)} %param.16) | copy-start | bytes 12292
  20.5 592.7 %copy-start.10 = (f32[2,512]{1,0:T(2,128)S(1)}, f32[2,512]{1,0:T(2,128)}, u32[]{:S(2)}) copy-start(f32[2,512]{1,0:T(2,128)} %param.17) | copy-start | bytes 12292
  20.5 608.0 %copy-start.4 = (f32[4,99,512]{2,1,0:T(8,128)S(1)}, f32[4,99,512]{2,1,0:T(8,128)}, u32[]{:S(2)}) copy-start(f32[4,99,512]{2,1,0:T(8,128)} %copy-done.3) | copy-start | bytes 2433028
  616.0 70.6 %all-to-all-start = ((bf16[512,2,512]{2,1,0:T(2,128)(2,1)}), bf16[512,2,512]{2,1,0:T(2,128)(2,1)S(1)}, u32[]{:S(2)}, u32[]{:S(2)}) async-start(bf16[512,2,512]{2,1,0:T(2,128)(2,1)} %stack.2), calls=%async_computation | async-start | bytes 2097152 | tf_op jit(solution)/shard_map/all_to_all | solution.py:53
Sparse Core Ops, SparseCore 0:
  20.6 487.1 all-reduce.3
